TPU v7x, 512 devices: a whole 4x4x16 slice. The times are simulated.
512 devices in a mesh: row: 32 (over z_hi, x, core), col: 16 (over y, z_lo).
Axes of the slice: x: 4, y: 4, z: 16 (z_hi: 4, z_lo: 4; z = z_hi * 4 + z_lo), core: 2. Of those that a mesh axis runs over, the one named last changes fastest.
Arguments:
- right_sides: float32 [8, 131072], P(None, ('row', 'col')), may hold values from -11 to 11
- noise_var: float32 [131072], P(('row', 'col')), may hold values from 1.2 to 3
- observed: int32 [131072], P(('row', 'col')), may hold values 0 or 1
- tile_data: bfloat16 [32, 16, 32, 128, 128], P('row', 'col'), may hold values from -1 to 1
- diag_tiles: bfloat16 [1024, 128, 128], P(('row', 'col')), may hold values from -1 to 1
- tile_rows: int32 [32, 16, 32], P('row', 'col'), may hold values from 0 to 63
- tile_cols: int32 [32, 16, 32], P('row', 'col'), may hold values from 0 to 31
- tile_count: int32 [32, 16], P('row', 'col'), may hold values from 16 to 32, as said below
Outputs:
- solution: float32 [8, 131072], P(None, ('row', 'col'))
- residual: float32 [8, 131072], P(None, ('row', 'col'))
Inputs may be any that keep to these rules, and one draw needn't show every extreme that they name: A device's slots t < tile_count name distinct pairs (i, j) whose blocks satisfy I != J, with I < J exactly when I + J is even, so that each pair of blocks is stored at most once; slots beyond the count hold arbitrary indices in range. Every device of the last row has exactly 32 live slots.
All inputs are finite; a program needn't handle non-finite values. No bound on the sum of `observed` on one device may be relied on, other than what follows from the above.
Results may differ from a plain program's by a relative error of at most 0.0003.
Values sent between devices are 32-bit elements; how exact they have to be, the bound alone decides.
A program may use at most 64 MiB of HBM per device.

v0:
```python
import math
import jax
import jax.numpy as jnp
from jax import lax
from jax.sharding import PartitionSpec as P

TILE = 128
COUPLED = 32
ITERS = 2


def residual_norms(residual):
    return lax.psum(jnp.sum(residual * residual, axis=1), ("row", "col"))


def local(
    right_sides, noise_var, observed, tile_data, diag_tiles, tile_rows, tile_cols, tile_count
):
    rhs_count = right_sides.shape[0]
    block_here = diag_tiles.shape[0]
    tile_size = diag_tiles.shape[1]
    piece_len = block_here * tile_size
    row_devices = lax.axis_size("row")
    col_devices = lax.axis_size("col")
    coupling = 1.0 / (2.0 * math.sqrt(TILE * (2 * COUPLED + 1)))
    highest = lax.Precision.HIGHEST
    observed_float = observed.astype(jnp.float32)[None, :]
    noise_row = noise_var[None, :]
    local_tiles = tile_data[0, 0].astype(jnp.float32)
    picks_row = tile_rows[0, 0]
    picks_col = tile_cols[0, 0]
    live_slots = jnp.arange(local_tiles.shape[0]) < tile_count[0, 0]
    row_hot = (
        (picks_row[:, None] == jnp.arange(row_devices * block_here)[None, :]) & live_slots[:, None]
    ).astype(jnp.float32)
    col_hot = (
        (picks_col[:, None] == jnp.arange(col_devices * block_here)[None, :]) & live_slots[:, None]
    ).astype(jnp.float32)
    row_index = jnp.arange(tile_size)[:, None]
    col_index = jnp.arange(tile_size)[None, :]
    diag_float = diag_tiles.astype(jnp.float32)
    zero_tiles = jnp.zeros_like(diag_float)
    diag_upper = jnp.where((col_index >= row_index)[None, :, :], diag_float, zero_tiles)
    diag_strict = jnp.where((col_index > row_index)[None, :, :], diag_float, zero_tiles)
    solution = jnp.zeros_like(right_sides)
    residual = right_sides
    direction = right_sides
    norm_now = residual_norms(residual)
    for iteration in range(ITERS):
        masked = observed_float * direction
        by_col = lax.all_gather(masked, "col", axis=1, tiled=True)
        by_row = lax.all_gather(masked, "row", axis=1, tiled=True)
        by_col = by_col.reshape(rhs_count, col_devices * block_here, tile_size)
        by_row = by_row.reshape(rhs_count, row_devices * block_here, tile_size)
        upper_terms = jnp.einsum(
            "tab,stb->sta", local_tiles, jnp.take(by_col, picks_col, axis=1), precision=highest
        )
        row_terms = jnp.einsum("sta,ti->sia", upper_terms, row_hot, precision=highest)
        own_rows = lax.psum_scatter(
            row_terms.reshape(rhs_count, row_devices * piece_len),
            "row",
            scatter_dimension=1,
            tiled=True,
        )
        lower_terms = jnp.einsum(
            "tab,sta->stb", local_tiles, jnp.take(by_row, picks_row, axis=1), precision=highest
        )
        col_terms = jnp.einsum("stb,tj->sjb", lower_terms, col_hot, precision=highest)
        mirrored = lax.psum_scatter(
            col_terms.reshape(rhs_count, col_devices * piece_len),
            "col",
            scatter_dimension=1,
            tiled=True,
        )
        local_blocks = masked.reshape(rhs_count, block_here, tile_size)
        diag_terms = jnp.einsum("kab,skb->ska", diag_upper, local_blocks, precision=highest)
        diag_terms = diag_terms + jnp.einsum(
            "kab,ska->skb", diag_strict, local_blocks, precision=highest
        )
        total = own_rows + mirrored + diag_terms.reshape(rhs_count, piece_len)
        image_field = noise_row * direction + observed_float * (coupling * total)
        step_alpha = norm_now / lax.psum(jnp.sum(direction * image_field, axis=1), ("row", "col"))
        solution = solution + step_alpha[:, None] * direction
        residual = residual - step_alpha[:, None] * image_field
        norm_next = residual_norms(residual)
        direction = residual + (norm_next / norm_now)[:, None] * direction
        norm_now = norm_next
    return (solution, residual)


def solution(mesh):
    return jax.shard_map(
        local,
        mesh=mesh,
        in_specs=(
            P(None, ("row", "col")),
            P(("row", "col")),
            P(("row", "col")),
            P("row", "col", None, None, None),
            P(("row", "col"), None, None),
            P("row", "col", None),
            P("row", "col", None),
            P("row", "col"),
        ),
        out_specs=(P(None, ("row", "col")), P(None, ("row", "col"))),
        check_vma=False,
    )
```

profile of v0, /device:TPU:1, one launch (start us, length us, event | category | flops | bytes accessed | tf_op | source)
XLA Modules:
  0.0 862.3 jit_solution(10460393890309216565)
XLA Ops:
  7.2 0.7 compare_select_fusion
  8.0 0.7 convert_element_type.4
  9.4 61.0 %all_gather.13 = f32[8,8192]{1,0:T(8,128)S(1)} all-gather(f32[8,256]{1,0:T(8,128)S(1)} %broadcast_multiply_fusion.1), channel_id=1, replica_groups=mesh['row'=32,'col'=16] {'row'}, dimensions={1}, use_global_device_ids=true | all-gather | bytes 270336 | tf_op jit(solution)/shard_map/all_gather | solution.py:52
  70.4 0.6 gather_fusion.1
  71.0 1.0 fusion.12
  72.0 0.7 copy-done.3
  72.9 0.7 copy.41
  73.7 35.8 %all_gather.12 = f32[8,4096]{1,0:T(8,128)S(1)} all-gather(f32[8,256]{1,0:T(8,128)S(1)} %broadcast_multiply_fusion.1), channel_id=1, replica_groups=mesh['row'=32,'col'=16] {'col'}, dimensions={1}, use_global_device_ids=true | all-gather | bytes 139264 | tf_op jit(solution)/shard_map/all_gather | solution.py:51
  109.5 0.6 gather_fusion
  110.1 1.8 fusion.14
  111.8 0.4 convolution_bitcast_fusion.1
  112.2 0.8 copy.39
  113.2 0.6 copy-done.2
  114.2 28.7 %reduce-scatter.7.cloned.1.call-done = f32[8,256]{1,0:T(8,128)} async-done(((f32[8,4096]{1,0:T(8,128)}), f32[8,256]{1,0:T(8,128)}) %reduce-scatter.7.cloned.1.call-update) | async-done | bytes 8208 | tf_op jit(solution)/shard_map/reduce_scatter | solution.py:69
  143.0 121.6 %reduce-scatter.5.cloned.1.call-done = f32[8,256]{1,0:T(8,128)} async-done(((f32[8,8192]{1,0:T(8,128)}), f32[8,256]{1,0:T(8,128)}) %reduce-scatter.5.cloned.1.call-update) | async-done | bytes 8208 | tf_op jit(solution)/shard_map/reduce_scatter | solution.py:59
  264.6 1.1 multiply_reduce_fusion.2
  265.7 101.8 %all-reduce = (f32[8]{0:T(128)S(1)}, f32[8]{0:T(128)S(1)}) all-reduce(f32[8]{0:T(128)S(1)} %get-tuple-element.5, f32[8]{0:T(128)S(1)} %get-tuple-element.4), channel_id=1, replica_groups=mesh['row'=32,'col'=16] {'row','col'}, use_global_device_ids=true, to_apply=%region_1.2 | all-reduce | flops 16 | bytes 128 | tf_op jit(solution)/shard_map/psum | solution.py:13
  367.6 100.1 %psum.30 = f32[8]{0:T(128)S(1)} all-reduce(f32[8]{0:T(128)S(1)} %multiply_reduce_fusion.1), channel_id=1, replica_groups=mesh['row'=32,'col'=16] {'row','col'}, use_global_device_ids=true, to_apply=%region_7.10 | all-reduce | flops 8 | bytes 64 | tf_op jit(solution)/shard_map/psum | solution.py:13
  467.9 34.1 %all_gather.14 = f32[8,4096]{1,0:T(8,128)S(1)} all-gather(f32[8,256]{1,0:T(8,128)S(1)} %get-tuple-element.8), channel_id=1, replica_groups=mesh['row'=32,'col'=16] {'col'}, dimensions={1}, use_global_device_ids=true | all-gather | bytes 139264 | tf_op jit(solution)/shard_map/all_gather | solution.py:51
  502.0 57.3 %all_gather.15 = f32[8,8192]{1,0:T(8,128)S(1)} all-gather(f32[8,256]{1,0:T(8,128)S(1)} %get-tuple-element.8), channel_id=1, replica_groups=mesh['row'=32,'col'=16] {'row'}, dimensions={1}, use_global_device_ids=true | all-gather | bytes 270336 | tf_op jit(solution)/shard_map/all_gather | solution.py:52
  559.3 0.6 gather_fusion.2
  559.9 0.6 gather_fusion.3
  560.5 1.0 fusion.8
  561.7 0.7 copy.40
  562.5 1.8 fusion.10
  564.2 0.4 convolution_bitcast_fusion
  564.6 0.8 copy.38
  565.8 64.8 %reduce-scatter.11.cloned.1.call-done = f32[8,256]{1,0:T(8,128)} async-done(((f32[8,4096]{1,0:T(8,128)}), f32[8,256]{1,0:T(8,128)}) %reduce-scatter.11.cloned.1.call-update) | async-done | bytes 8208 | tf_op jit(solution)/shard_map/reduce_scatter | solution.py:69
  630.7 121.7 %reduce-scatter.9.cloned.1.call-done = f32[8,256]{1,0:T(8,128)} async-done(((f32[8,8192]{1,0:T(8,128)}), f32[8,256]{1,0:T(8,128)}) %reduce-scatter.9.cloned.1.call-update) | async-done | bytes 8208 | tf_op jit(solution)/shard_map/reduce_scatter | solution.py:59
  752.3 1.0 multiply_reduce_fusion
  753.4 101.7 %psum.31 = f32[8]{0:T(128)S(1)} all-reduce(f32[8]{0:T(128)S(1)} %get-tuple-element.13), channel_id=1, replica_groups=mesh['row'=32,'col'=16] {'row','col'}, use_global_device_ids=true, to_apply=%region_11.14 | all-reduce | flops 8 | bytes 64 | tf_op jit(solution)/shard_map/psum | solution.py:82
  855.1 0.7 multiply_subtract_fusion
  (39 shorter events, 1.7 us)
Async XLA Ops:
  7.2 63.8 %copy-start = (bf16[1,1,32,128,128]{4,3,2,1,0:T(8,128)(2,1)S(1)}, bf16[1,1,32,128,128]{4,3,2,1,0:T(8,128)(2,1)}, u32[]{:S(2)}) copy-start(bf16[1,1,32,128,128]{4,3,2,1,0:T(8,128)(2,1)} %param.15) | copy-start | bytes 3145732
  7.2 0.8 copy-start.4
  7.2 2.2 copy-start.1
  7.2 135.8 %reduce-scatter.7.cloned.1.call-start = ((), (), s32[]{:S(2)}) async-start(), calls=%async_computation.5 | async-start | bytes 139264 | tf_op jit(solution)/shard_map/reduce_scatter | solution.py:69
  72.0 0.7 copy-start.3
  73.6 191.0 %reduce-scatter.5.cloned.1.call-start = ((), (), s32[]{:S(2)}) async-start(), calls=%async_computation.4 | async-start | bytes 270336 | tf_op jit(solution)/shard_map/reduce_scatter | solution.py:59
  113.1 0.7 copy-start.2
  113.1 0.9 copy-start.5
  113.1 517.5 %reduce-scatter.11.cloned.1.call-start = ((), (), s32[]{:S(2)}) async-start(), calls=%async_computation.7 | async-start | bytes 139264 | tf_op jit(solution)/shard_map/reduce_scatter | solution.py:69
  114.0 150.6 %copy-start.6 = (f32[256]{0:T(256)S(1)}, f32[256]{0:T(256)}, u32[]{:S(2)}) copy-start(f32[256]{0:T(256)} %param.13) | copy-start | bytes 3076
  562.4 189.9 %reduce-scatter.9.cloned.1.call-start = ((), (), s32[]{:S(2)}) async-start(), calls=%async_computation.6 | async-start | bytes 270336 | tf_op jit(solution)/shard_map/reduce_scatter | solution.py:59
Sparse Core Ops, SparseCore 0:
  73.7 69.1 reduce-scatter.6
  147.3 117.2 reduce-scatter.4
  562.5 68.0 reduce-scatter.10
  634.8 117.4 reduce-scatter.8
where the time goes:
time: 863 us; the launch traced here: 862 us
  blocking collectives  492 us (57%)
  waiting for transfers between devices  337 us (39%)
  between operations  14.6 us (2%)
  matrix products  9.38 us (1%)
    reduce_scatter x2, waiting for transfers between devices, local(): lax.psum_scatter(row_terms.reshape(rhs_count, row_devices * piece_len), '...  243 us
    psum x2, blocking collectives, residual_norms(): return lax.psum(jnp.sum(residual * residual, axis=1), ('row', 'col'))  202 us
    all_gather x2, blocking collectives, local(): by_row = lax.all_gather(masked, 'row', axis=1, tiled=True)  118 us
    psum x1, blocking collectives, local(): lax.psum(jnp.sum(direction * image_field, axis=1), ('row', 'col'))  102 us
    reduce_scatter x2, waiting for transfers between devices, local(): lax.psum_scatter(col_terms.reshape(rhs_count, col_devices * piece_len), '...  93.6 us
    all_gather x2, blocking collectives, local(): by_col = lax.all_gather(masked, 'col', axis=1, tiled=True)  69.9 us
  transfers between devices with their start and end apart: 4, of which 4 were waited for; matrix products, arithmetic and copies ran while one was open for 1% of the time, Pallas kernels for 0%

commit v1 on v0

--- a/solution.py
+++ b/solution.py
@@ -3,6 +3,7 @@
 import jax.numpy as jnp
 from jax import lax
 from jax.sharding import PartitionSpec as P
+from jax.lax import psum
 
 TILE = 128
 COUPLED = 32
@@ -79,7 +80,8 @@
         )
         total = own_rows + mirrored + diag_terms.reshape(rhs_count, piece_len)
         image_field = noise_row * direction + observed_float * (coupling * total)
-        step_alpha = norm_now / lax.psum(jnp.sum(direction * image_field, axis=1), ("row", "col"))
+        lots_all_group = lambda t0: psum(psum(t0, axis_name="row"), axis_name="col")
+        step_alpha = norm_now / lots_all_group(jnp.sum(direction * image_field, axis=1))
         solution = solution + step_alpha[:, None] * direction
         residual = residual - step_alpha[:, None] * image_field
         norm_next = residual_norms(residual)

time: 863 us -> 1010 us (1.17)
  blocking collectives: 492 us -> 636 us
    psum x1 -> x4, blocking collectives: 102 us -> 239 us  [local(): lots_all_group = lambda t0: psum(psum(t0, axis_name='row'), axis_name='col')]
where the time goes in v1:
time: 1010 us
  blocking collectives  636 us (63%)
  waiting for transfers between devices  337 us (33%)
  between operations  14.6 us (1%)
    reduce_scatter x2, waiting for transfers between devices, local(): lax.psum_scatter(row_terms.reshape(rhs_count, row_devices * piece_len), '...  243 us
    psum x4, blocking collectives, local(): lots_all_group = lambda t0: psum(psum(t0, axis_name='row'), axis_name='col')  239 us
    psum x2, blocking collectives, residual_norms(): return lax.psum(jnp.sum(residual * residual, axis=1), ('row', 'col'))  208 us
    all_gather x2, blocking collectives, local(): by_row = lax.all_gather(masked, 'row', axis=1, tiled=True)  119 us
    reduce_scatter x2, waiting for transfers between devices, local(): lax.psum_scatter(col_terms.reshape(rhs_count, col_devices * piece_len), '...  93.6 us
    all_gather x2, blocking collectives, local(): by_col = lax.all_gather(masked, 'col', axis=1, tiled=True)  69.9 us
  transfers between devices with their start and end apart: 4, of which 4 were waited for; matrix products, arithmetic and copies ran while one was open for 1% of the time, Pallas kernels for 0%

profile of v1, /device:TPU:1, one launch (start us, length us, event | category | flops | bytes accessed | tf_op | source)
XLA Modules:
  0.0 1006.1 jit_solution(18148739617973903369)
XLA Ops:
  7.2 0.7 compare_select_fusion
  8.0 0.7 convert_element_type.4
  9.4 61.0 %all_gather.13 = f32[8,8192]{1,0:T(8,128)S(1)} all-gather(f32[8,256]{1,0:T(8,128)S(1)} %broadcast_multiply_fusion.1), channel_id=1, replica_groups=mesh['row'=32,'col'=16] {'row'}, dimensions={1}, use_global_device_ids=true | all-gather | bytes 270336 | tf_op jit(solution)/shard_map/all_gather | solution.py:53
  70.4 0.6 gather_fusion.1
  71.0 1.0 fusion.12
  72.0 0.7 copy-done.3
  72.9 0.7 copy.41
  73.7 35.8 %all_gather.12 = f32[8,4096]{1,0:T(8,128)S(1)} all-gather(f32[8,256]{1,0:T(8,128)S(1)} %broadcast_multiply_fusion.1), channel_id=1, replica_groups=mesh['row'=32,'col'=16] {'col'}, dimensions={1}, use_global_device_ids=true | all-gather | bytes 139264 | tf_op jit(solution)/shard_map/all_gather | solution.py:52
  109.5 0.6 gather_fusion
  110.1 1.8 fusion.14
  112.2 0.8 copy.39
  113.2 0.6 copy-done.2
  114.2 28.7 %reduce-scatter.7.cloned.1.call-done = f32[8,256]{1,0:T(8,128)} async-done(((f32[8,4096]{1,0:T(8,128)}), f32[8,256]{1,0:T(8,128)}) %reduce-scatter.7.cloned.1.call-update) | async-done | bytes 8208 | tf_op jit(solution)/shard_map/reduce_scatter | solution.py:70
  143.0 121.6 %reduce-scatter.5.cloned.1.call-done = f32[8,256]{1,0:T(8,128)} async-done(((f32[8,8192]{1,0:T(8,128)}), f32[8,256]{1,0:T(8,128)}) %reduce-scatter.5.cloned.1.call-update) | async-done | bytes 8208 | tf_op jit(solution)/shard_map/reduce_scatter | solution.py:60
  264.6 1.1 multiply_reduce_fusion.2
  265.7 86.3 %psum.43 = f32[8]{0:T(128)S(1)} all-reduce(f32[8]{0:T(128)S(1)} %get-tuple-element.4), channel_id=1, replica_groups=mesh['row'=32,'col'=16] {'row'}, use_global_device_ids=true, to_apply=%region_5.8 | all-reduce | flops 8 | bytes 64 | tf_op jit(solution)/shard_map/psum | solution.py:83
  352.0 102.3 %psum.42 = f32[8]{0:T(128)S(1)} all-reduce(f32[8]{0:T(128)S(1)} %get-tuple-element.5), channel_id=1, replica_groups=mesh['row'=32,'col'=16] {'row','col'}, use_global_device_ids=true, to_apply=%region_1.2 | all-reduce | flops 8 | bytes 64 | tf_op jit(solution)/shard_map/psum | solution.py:14
  454.2 32.8 %psum.44 = f32[8]{0:T(128)S(1)} all-reduce(f32[8]{0:T(128)S(1)} %psum.43), channel_id=1, replica_groups=mesh['row'=32,'col'=16] {'col'}, use_global_device_ids=true, to_apply=%region_6.9 | all-reduce | flops 8 | bytes 64 | tf_op jit(solution)/shard_map/psum | solution.py:83
  487.2 105.6 %psum.45 = f32[8]{0:T(128)S(1)} all-reduce(f32[8]{0:T(128)S(1)} %multiply_reduce_fusion.1), channel_id=1, replica_groups=mesh['row'=32,'col'=16] {'row','col'}, use_global_device_ids=true, to_apply=%region_8.11 | all-reduce | flops 8 | bytes 64 | tf_op jit(solution)/shard_map/psum | solution.py:14
  592.9 34.1 %all_gather.14 = f32[8,4096]{1,0:T(8,128)S(1)} all-gather(f32[8,256]{1,0:T(8,128)S(1)} %get-tuple-element.6), channel_id=1, replica_groups=mesh['row'=32,'col'=16] {'col'}, dimensions={1}, use_global_device_ids=true | all-gather | bytes 139264 | tf_op jit(solution)/shard_map/all_gather | solution.py:52
  627.0 57.5 %all_gather.15 = f32[8,8192]{1,0:T(8,128)S(1)} all-gather(f32[8,256]{1,0:T(8,128)S(1)} %get-tuple-element.6), channel_id=1, replica_groups=mesh['row'=32,'col'=16] {'row'}, dimensions={1}, use_global_device_ids=true | all-gather | bytes 270336 | tf_op jit(solution)/shard_map/all_gather | solution.py:53
  685.1 0.6 gather_fusion.3
  685.7 1.0 fusion.8
  686.9 0.7 copy.40
  687.7 1.8 fusion.10
  689.9 0.8 copy.38
  691.0 64.9 %reduce-scatter.11.cloned.1.call-done = f32[8,256]{1,0:T(8,128)} async-done(((f32[8,4096]{1,0:T(8,128)}), f32[8,256]{1,0:T(8,128)}) %reduce-scatter.11.cloned.1.call-update) | async-done | bytes 8208 | tf_op jit(solution)/shard_map/reduce_scatter | solution.py:70
  755.9 121.6 %reduce-scatter.9.cloned.1.call-done = f32[8,256]{1,0:T(8,128)} async-done(((f32[8,8192]{1,0:T(8,128)}), f32[8,256]{1,0:T(8,128)}) %reduce-scatter.9.cloned.1.call-update) | async-done | bytes 8208 | tf_op jit(solution)/shard_map/reduce_scatter | solution.py:60
  877.6 1.0 multiply_reduce_fusion
  878.6 86.3 %psum.46 = f32[8]{0:T(128)S(1)} all-reduce(f32[8]{0:T(128)S(1)} %get-tuple-element.11), channel_id=1, replica_groups=mesh['row'=32,'col'=16] {'row'}, use_global_device_ids=true, to_apply=%region_12.15 | all-reduce | flops 8 | bytes 64 | tf_op jit(solution)/shard_map/psum | solution.py:83
  965.0 33.9 %psum.47 = f32[8]{0:T(128)S(1)} all-reduce(f32[8]{0:T(128)S(1)} %psum.46), channel_id=1, replica_groups=mesh['row'=32,'col'=16] {'col'}, use_global_device_ids=true, to_apply=%region_13.16 | all-reduce | flops 8 | bytes 64 | tf_op jit(solution)/shard_map/psum | solution.py:83
  998.8 0.7 multiply_subtract_fusion
  (42 shorter events, 3.1 us)
Async XLA Ops:
  7.2 63.8 %copy-start = (bf16[1,1,32,128,128]{4,3,2,1,0:T(8,128)(2,1)S(1)}, bf16[1,1,32,128,128]{4,3,2,1,0:T(8,128)(2,1)}, u32[]{:S(2)}) copy-start(bf16[1,1,32,128,128]{4,3,2,1,0:T(8,128)(2,1)} %param.15) | copy-start | bytes 3145732
  7.2 0.8 copy-start.4
  7.2 2.2 copy-start.1
  7.2 135.8 %reduce-scatter.7.cloned.1.call-start = ((), (), s32[]{:S(2)}) async-start(), calls=%async_computation.5 | async-start | bytes 139264 | tf_op jit(solution)/shard_map/reduce_scatter | solution.py:70
  72.0 0.7 copy-start.3
  73.6 191.0 %reduce-scatter.5.cloned.1.call-start = ((), (), s32[]{:S(2)}) async-start(), calls=%async_computation.4 | async-start | bytes 270336 | tf_op jit(solution)/shard_map/reduce_scatter | solution.py:60
  113.1 0.7 copy-start.2
  113.1 0.9 copy-start.5
  113.1 642.8 %reduce-scatter.11.cloned.1.call-start = ((), (), s32[]{:S(2)}) async-start(), calls=%async_computation.7 | async-start | bytes 139264 | tf_op jit(solution)/shard_map/reduce_scatter | solution.py:70
  114.0 150.6 %copy-start.6 = (f32[256]{0:T(256)S(1)}, f32[256]{0:T(256)}, u32[]{:S(2)}) copy-start(f32[256]{0:T(256)} %param.13) | copy-start | bytes 3076
  687.7 189.9 %reduce-scatter.9.cloned.1.call-start = ((), (), s32[]{:S(2)}) async-start(), calls=%async_computation.6 | async-start | bytes 270336 | tf_op jit(solution)/shard_map/reduce_scatter | solution.py:60
Sparse Core Ops, SparseCore 0:
  73.7 69.1 reduce-scatter.6
  147.3 117.2 reduce-scatter.4
  687.8 68.1 reduce-scatter.10
  760.1 117.4 reduce-scatter.8
